TPU v7x, 256 devices: a whole 4x4x8 slice. The times are simulated.
256 devices in a mesh: lat: 8 (over x, core), lon: 32 (over z, y).
Axes of the slice: x: 4, y: 4, z: 8, core: 2. Of those that a mesh axis runs over, the one named last changes fastest.
Arguments:
- latent: bfloat16 [64, 8192, 128], P('lat', 'lon'), may hold values from -6 to 6
- head: bfloat16 [128, 32], replicated, may hold values from -0.5 to 0.5
- bias: float32 [32], replicated, may hold values from -3 to 3
- targets: bfloat16 [32, 64, 4096], P(None, 'lat', 'lon'), may hold values from -6 to 6
- margin_cell: int32 [8, 32, 6144], P('lat', 'lon'), may hold values from 0 to 2047
- margin_pixel: int32 [8, 32, 6144], P('lat', 'lon'), may hold values from 0 to 2047, as said below
- margin_weight: float32 [8, 32, 6144], P('lat', 'lon'), may hold values from 0.05 to 1
- live_count: int32 [8, 32], P('lat', 'lon'), may hold values from 2457 to 6144, as said below
Outputs:
- latent_grad: bfloat16 [64, 8192, 128], P('lat', 'lon')
- head_grad: float32 [128, 32], replicated
- bias_grad: float32 [32], replicated
Inputs may be any that keep to these rules, and one draw needn't show every extreme that they name: `margin_pixel`: A tile pixel in the device's own band: tile row times (256) plus q, where q - 64 is the column relative to the device's own sector, so q < 64 and q >= 192 are the neighbouring sectors' columns. Both 0 and the largest value occur in every device's list; columns near the frame's edges are covered thinly or not at all. `live_count`: rows at or beyond a device's count are padding and are ignored; in every draw some device has all 6144 rows live.
All inputs are finite; a program needn't handle non-finite values.
Results may differ from a plain program's by a relative error of at most 0.0052.
Values may be sent and summed in bfloat16 or wider, within the bound.
A program may use at most 64 MiB of HBM per device.

v0:
```python
import math

import jax
import jax.numpy as jnp
from jax import lax
from jax.sharding import Mesh
from jax.sharding import PartitionSpec as P

LON = ("lon_0", "lon_1")
LAT_LON = ("lat_0", "lat_1", "lon_0", "lon_1")
LAT = ("lat_0", "lat_1")


def from_behind(shard, axis, by):
    devices = lax.axis_size(axis)
    return lax.ppermute(shard, axis, [(i, (i + by) % devices) for i in range(devices)])


def with_halo(cells, sides, width):
    for axis, dim in sides:
        count = lax.axis_size(axis)
        head = lax.slice_in_dim(cells, 0, width, axis=dim)
        tail = lax.slice_in_dim(cells, cells.shape[dim] - width, cells.shape[dim], axis=dim)
        cells = jnp.concatenate(
            [
                lax.ppermute(tail, axis, [(i, (i + 1) % count) for i in range(count)]),
                cells,
                lax.ppermute(head, axis, [((i + 1) % count, i) for i in range(count)]),
            ],
            axis=dim,
        )
    return cells


def by_axis(shard, axes):
    for axis in axes:
        shard = lax.psum(shard, axis)
    return shard


def accumulate(step_fn, initial, row_total):
    return step_fn(initial, 0, row_total)


def per_device(latent, head, bias, targets, margin_cell, margin_pixel, margin_weight, live_count):
    cycle_count, cycle_cells, latent_width = latent.shape
    cell_total = cycle_count * cycle_cells
    latent_rows = latent.reshape(cell_total, latent_width)
    var_count, tile_rows, tile_cols = targets.shape
    rim_width = tile_cols // 2
    frame_width = tile_cols + 2 * rim_width
    cell_ids = margin_cell.reshape(-1)
    pixel_ids = margin_pixel.reshape(-1)
    row_total = cell_ids.shape[0]
    live_total = live_count.reshape(())
    row_index = jnp.arange(row_total, dtype=jnp.int32)
    live_weight = jnp.where(row_index < live_total, margin_weight.reshape(-1), jnp.float32(0.0))
    predicted = (
        lax.dot_general(
            head, latent_rows, (((0,), (1,)), ((), ())), preferred_element_type=jnp.float32
        )
        + bias[:, None]
    ).astype(jnp.bfloat16)

    def spread(totals, first_row, row_span):
        contribution = (
            jnp.take(predicted, cell_ids, axis=1).astype(jnp.float32) * live_weight[None, :]
        )
        return totals.at[:, pixel_ids].add(contribution)

    frame_totals = accumulate(
        spread, jnp.zeros((var_count, tile_rows * frame_width), jnp.float32), row_total
    )
    frame = frame_totals.reshape(var_count, tile_rows, frame_width)
    west_strip = frame[:, :, :rim_width]
    own_part = frame[:, :, rim_width : rim_width + tile_cols]
    east_strip = frame[:, :, rim_width + tile_cols :]
    from_east = from_behind(west_strip, LON, -1)
    from_west = from_behind(east_strip, LON, 1)
    own_tiles = own_part.at[:, :, tile_cols - rim_width :].add(from_east)
    own_tiles = own_tiles.at[:, :, :rim_width].add(from_west)
    partial_frame = with_halo(own_part, ((LON, 2),), rim_width)
    target_frame = with_halo(targets, ((LON, 2),), rim_width)
    total_frame = jnp.concatenate(
        [
            west_strip + partial_frame[:, :, :rim_width],
            own_tiles,
            east_strip + partial_frame[:, :, rim_width + tile_cols :],
        ],
        axis=2,
    )
    misfit_frame = total_frame - target_frame.astype(jnp.float32)
    misfit_flat = misfit_frame.reshape(var_count, tile_rows * frame_width)

    def gather_back(totals, first_row, row_span):
        contribution = jnp.take(misfit_flat, pixel_ids, axis=1) * live_weight[None, :]
        return totals.at[:, cell_ids].add(contribution)

    cell_totals = accumulate(
        gather_back, jnp.zeros((var_count, cell_total), jnp.float32), row_total
    )
    cell_misfit = cell_totals.astype(jnp.bfloat16)
    latent_grad = lax.dot_general(
        cell_misfit, head, (((0,), (1,)), ((), ())), preferred_element_type=jnp.float32
    ).astype(jnp.bfloat16)
    head_part = lax.dot_general(
        latent_rows, cell_misfit, (((0,), (1,)), ((), ())), preferred_element_type=jnp.float32
    )
    bias_part = jnp.sum(cell_misfit.astype(jnp.float32), axis=1)
    head_total, bias_total = (by_axis(head_part, LAT_LON), by_axis(bias_part, LAT_LON))
    grad_scale = 1.0 / math.sqrt(cell_total * lax.axis_size(LAT) * lax.axis_size(LON))
    return (
        latent_grad.reshape(cycle_count, cycle_cells, latent_width),
        head_total * grad_scale,
        bias_total * grad_scale,
    )


def solution(mesh):
    split = Mesh(mesh.devices.reshape(4, 2, 8, 4), ("lat_0", "lat_1", "lon_0", "lon_1"))
    in_specs = (
        P(LAT, LON, None),
        P(),
        P(),
        P(None, LAT, LON),
        P(LAT, LON, None),
        P(LAT, LON, None),
        P(LAT, LON, None),
        P(LAT, LON),
    )
    out_specs = (P(LAT, LON, None), P(), P())
    return jax.shard_map(
        per_device, mesh=split, in_specs=in_specs, out_specs=out_specs, check_vma=False
    )
```

profile of v0, /device:TPU:4, one launch (start us, length us, event | category | flops | bytes accessed | tf_op | source)
XLA Modules:
  0.0 207.9 jit_solution(8948927558350395939)
XLA Ops:
  0.7 1.0 fusion.22
  1.7 1.7 collective-permute-start.4
  3.3 6.8 %collective-permute-start.5 = (bf16[32,8,64]{2,1,0:T(8,128)(2,1)S(1)}, bf16[32,8,64]{2,1,0:T(8,128)(2,1)S(1)}, u32[]{:S(2)}, u32[]{:S(2)}) collective-permute-start(bf16[32,8,64]{2,1,0:T(8,128)(2,1)S(1)} %get-tuple-element.40), channel_id=1, source_target_pairs={{1,0},{2,1},{3,2},{4,3},{5,4},{6,5},{7,6},{8,7},{9,8},{10,9},{11,1... | collective-permute-start | bytes 98312 | tf_op jit(solution)/shard_map/ppermute | solution.py:28
  10.8 0.8 compare_select_fusion.1
  11.6 0.8 compare_and_fusion
  12.3 0.8 compare_select_fusion
  13.1 1.0 fusion.6
  14.1 0.3 copy.18
  14.4 56.4 %scatter_custom_fusion = f32[32,2048]{0,1:T(8,128)S(1)} fusion(s32[6144]{0:T(1024)S(1)} %bitcast.29, f32[6144]{0:T(1024)S(1)} %fusion.16, pred[6144]{0:T(1024)(128)(4,1)S(1)} %compare_and_fusion, bf16[]{:T(256)} %constant.87.clone.1, f32[]{:T(128)} %constant.83.clone.1, bf16[32,2048]{0,1:T(8,128)(2,1)S(1)} %copy.18, s32[6144]{0:T(1024)S(1)} %broadcast_clamp_fusion.1), kind=kCustom, calls=%fused_computation.4 | custom fusion | flops 786432 | bytes 841734 | tf_op jit(solution)/shard_map/scatter-add | solution.py:69
  71.0 0.1 copy.29
  71.1 2.0 collective-permute-start.3
  73.3 0.2 collective-permute-start.2
  73.6 5.3 %collective-permute-start.1 = (f32[32,8,64]{2,1,0:T(8,128)S(1)}, f32[32,8,64]{2,1,0:T(8,128)S(1)}, u32[]{:S(2)}, u32[]{:S(2)}) collective-permute-start(f32[32,8,64]{2,1,0:T(8,128)S(1)} %copy.25), channel_id=1, source_target_pairs={{0,31},{1,0},{2,1},{3,2},{4,3},{5,4},{6,5},{7,6},{8,7},{9,8},{10,9... | collective-permute-start | bytes 196616 | tf_op jit(solution)/shard_map/ppermute | solution.py:16
  79.0 0.2 copy.27
  79.2 0.1 copy.26
  79.3 2.1 %collective-permute-done.1 = f32[32,8,64]{2,1,0:T(8,128)S(1)} collective-permute-done((f32[32,8,64]{2,1,0:T(8,128)S(1)}, f32[32,8,64]{2,1,0:T(8,128)S(1)}, u32[]{:S(2)}, u32[]{:S(2)}) %collective-permute-start.1) | collective-permute-done | bytes 65568 | tf_op jit(solution)/shard_map/ppermute | solution.py:16
  81.5 4.8 %scatter-add.25 = f32[32,8,128]{2,1,0:T(8,128)S(1)} dynamic-update-slice(f32[32,8,128]{2,1,0:T(8,128)S(1)} %copy.27, f32[32,8,64]{2,1,0:T(8,128)S(1)} %add.91, s32[]{:T(128)} %constant.84.clone.1, s32[]{:T(128)} %constant.84.clone.1, s32[]{:T(128)} %constant.88.clone.1) | dynamic-update-slice | bytes 131076 | tf_op jit(solution)/shard_map/scatter-add | solution.py:80
  86.3 0.5 scatter-add.26
  86.8 3.4 %collective-permute-done = f32[32,8,64]{2,1,0:T(8,128)S(1)} collective-permute-done((f32[32,8,64]{2,1,0:T(8,128)S(1)}, f32[32,8,64]{2,1,0:T(8,128)S(1)}, u32[]{:S(2)}, u32[]{:S(2)}) %collective-permute-start) | collective-permute-done | bytes 65568 | tf_op jit(solution)/shard_map/ppermute | solution.py:26
  90.2 0.2 maximum_subtract_fusion
  90.4 0.4 copy.24
  90.8 51.0 %scatter_custom_fusion.1 = f32[32,2048]{0,1:T(8,128)S(1)} fusion(s32[6144]{0:T(1024)S(1)} %bitcast.28, f32[6144]{0:T(1024)S(1)} %fusion.16, f32[]{:T(128)} %constant.89.clone.1, pred[6144]{0:T(1024)(128)(4,1)S(1)} %compare_and_fusion.1, f32[]{:T(128)} %constant.83.clone.1, f32[32,2048]{0,1:T(8,128)S(1)} %bitcast.25, s32[6144]{0:T(1024)S(1)} %broadcast_clamp_fusion), kind=kCustom, calls=%fused_computation.6 | custom fusion | flops 589824 | bytes 1366024 | tf_op jit(solution)/shard_map/scatter-add | solution.py:97
  141.8 0.3 convert_reduce_fusion
  142.1 0.3 convolution_bitcast_fusion
  142.4 0.4 copy-done.3
  142.8 1.1 convolution_convert_fusion
  143.8 15.4 %all-reduce.2 = (f32[128,32]{0,1:T(8,128)S(1)}, f32[32]{0:T(128)S(1)}) all-reduce(f32[128,32]{0,1:T(8,128)S(1)} %convolution_bitcast_fusion, f32[32]{0:T(128)S(1)} %convert_reduce_fusion), channel_id=1, replica_groups=mesh['lat_0'=4,'lat_1'=2,'lon_0'=8,'lon_1'=4] {'lat_0'}, use_global_device_ids=true, to_apply=%region_2.3 | all-reduce | flops 4128 | bytes 33024 | tf_op jit(solution)/shard_map/psum | solution.py:37
  159.3 3.4 %all-reduce.3 = (f32[128,32]{0,1:T(8,128)S(1)}, f32[32]{0:T(128)S(1)}) all-reduce(f32[128,32]{0,1:T(8,128)S(1)} %get-tuple-element.31, f32[32]{0:T(128)S(1)} %get-tuple-element.32), channel_id=1, replica_groups=mesh['lat_0'=4,'lat_1'=2,'lon_0'=8,'lon_1'=4] {'lat_1'}, use_global_device_ids=true, to_apply=%region_3.4 | all-reduce | flops 4128 | bytes 33024 | tf_op jit(solution)/shard_map/psum | solution.py:37
  162.7 27.1 %all-reduce = (f32[128,32]{0,1:T(8,128)S(1)}, f32[32]{0:T(128)S(1)}) all-reduce(f32[128,32]{0,1:T(8,128)S(1)} %get-tuple-element.33, f32[32]{0:T(128)S(1)} %get-tuple-element.34), channel_id=1, replica_groups=mesh['lat_0'=4,'lat_1'=2,'lon_0'=8,'lon_1'=4] {'lon_0'}, use_global_device_ids=true, to_apply=%region_4.5 | all-reduce | flops 4128 | bytes 33024 | tf_op jit(solution)/shard_map/psum | solution.py:37
  189.7 17.0 %all-reduce.1 = (f32[128,32]{0,1:T(8,128)S(1)}, f32[32]{0:T(128)S(1)}) all-reduce(f32[128,32]{0,1:T(8,128)S(1)} %get-tuple-element.27, f32[32]{0:T(128)S(1)} %get-tuple-element.28), channel_id=1, replica_groups=mesh['lat_0'=4,'lat_1'=2,'lon_0'=8,'lon_1'=4] {'lon_1'}, use_global_device_ids=true, to_apply=%region_5.6 | all-reduce | flops 4128 | bytes 33024 | tf_op jit(solution)/shard_map/psum | solution.py:37
  206.7 0.6 broadcast_multiply_fusion
  207.4 0.5 broadcast_multiply_fusion.1
  (26 shorter events, 0.5 us)
Async XLA Ops:
  0.6 12.5 %copy-start = (bf16[8,256,128]{2,1,0:T(8,128)(2,1)S(1)}, bf16[8,256,128]{2,1,0:T(8,128)(2,1)}, u32[]{:S(2)}) copy-start(bf16[8,256,128]{2,1,0:T(8,128)(2,1)} %param.12) | copy-start | bytes 1572868
  0.6 13.7 %copy-start.4 = (f32[1,1,6144]{2,1,0:T(1,128)S(1)}, f32[1,1,6144]{2,1,0:T(1,128)}, u32[]{:S(2)}) copy-start(f32[1,1,6144]{2,1,0:T(1,128)} %param.18) | copy-start | bytes 73732
  1.7 88.5 %collective-permute-start.4 = (bf16[32,8,64]{2,1,0:T(8,128)(2,1)S(1)}, bf16[32,8,64]{2,1,0:T(8,128)(2,1)S(1)}, u32[]{:S(2)}, u32[]{:S(2)}) collective-permute-start(bf16[32,8,64]{2,1,0:T(8,128)(2,1)S(1)} %get-tuple-element.39), channel_id=1, source_target_pairs={{0,1},{1,2},{2,3},{3,4},{4,5},{5,6},{6,7},{7,8},{8,9},{9,10},{10,1... | collective-permute-start | bytes 98312 | tf_op jit(solution)/shard_map/ppermute | solution.py:26
  3.3 86.8 %collective-permute-start.5 = (bf16[32,8,64]{2,1,0:T(8,128)(2,1)S(1)}, bf16[32,8,64]{2,1,0:T(8,128)(2,1)S(1)}, u32[]{:S(2)}, u32[]{:S(2)}) collective-permute-start(bf16[32,8,64]{2,1,0:T(8,128)(2,1)S(1)} %get-tuple-element.40), channel_id=1, source_target_pairs={{1,0},{2,1},{3,2},{4,3},{5,4},{6,5},{7,6},{8,7},{9,8},{10,9},{11,1... | collective-permute-start | bytes 98312 | tf_op jit(solution)/shard_map/ppermute | solution.py:28
  71.0 8.0 %copy-start.2 = (s32[1,1,6144]{2,1,0:T(1,128)S(1)}, s32[1,1,6144]{2,1,0:T(1,128)}, u32[]{:S(2)}) copy-start(s32[1,1,6144]{2,1,0:T(1,128)} %param.17) | copy-start | bytes 73732
  71.1 15.6 %collective-permute-start.3 = (f32[32,8,64]{2,1,0:T(8,128)S(1)}, f32[32,8,64]{2,1,0:T(8,128)S(1)}, u32[]{:S(2)}, u32[]{:S(2)}) collective-permute-start(f32[32,8,64]{2,1,0:T(8,128)S(1)} %copy.29), channel_id=1, source_target_pairs={{1,0},{2,1},{3,2},{4,3},{5,4},{6,5},{7,6},{8,7},{9,8},{10,9},{11,1... | collective-permute-start | bytes 196616 | tf_op jit(solution)/shard_map/ppermute | solution.py:28
  73.3 13.0 %collective-permute-start.2 = (f32[32,8,64]{2,1,0:T(8,128)S(1)}, f32[32,8,64]{2,1,0:T(8,128)S(1)}, u32[]{:S(2)}, u32[]{:S(2)}) collective-permute-start(f32[32,8,64]{2,1,0:T(8,128)S(1)} %copy.28), channel_id=1, source_target_pairs={{0,1},{1,2},{2,3},{3,4},{4,5},{5,6},{6,7},{7,8},{8,9},{9,10},{10,1... | collective-permute-start | bytes 196616 | tf_op jit(solution)/shard_map/ppermute | solution.py:16
  73.6 7.9 %collective-permute-start.1 = (f32[32,8,64]{2,1,0:T(8,128)S(1)}, f32[32,8,64]{2,1,0:T(8,128)S(1)}, u32[]{:S(2)}, u32[]{:S(2)}) collective-permute-start(f32[32,8,64]{2,1,0:T(8,128)S(1)} %copy.25), channel_id=1, source_target_pairs={{0,31},{1,0},{2,1},{3,2},{4,3},{5,4},{6,5},{7,6},{8,7},{9,8},{10,9... | collective-permute-start | bytes 196616 | tf_op jit(solution)/shard_map/ppermute | solution.py:16
  79.3 10.9 %copy-start.1 = (bf16[32,8,128]{2,1,0:T(8,128)(2,1)S(1)}, bf16[32,8,128]{2,1,0:T(8,128)(2,1)}, u32[]{:S(2)}) copy-start(bf16[32,8,128]{2,1,0:T(8,128)(2,1)} %param.15) | copy-start | bytes 196612
  81.4 8.7 %collective-permute-start = (f32[32,8,64]{2,1,0:T(8,128)S(1)}, f32[32,8,64]{2,1,0:T(8,128)S(1)}, u32[]{:S(2)}, u32[]{:S(2)}) collective-permute-start(f32[32,8,64]{2,1,0:T(8,128)S(1)} %copy.26), channel_id=1, source_target_pairs={{0,1},{1,2},{2,3},{3,4},{4,5},{5,6},{6,7},{7,8},{8,9},{9,10},{10,1... | collective-permute-start | bytes 196616 | tf_op jit(solution)/shard_map/ppermute | solution.py:26
  142.1 0.7 copy-start.3
where the time goes:
time: 208 us
  other arithmetic  111 us (53%)
  blocking collectives  62.9 us (30%)
  starting transfers between devices  16 us (8%)
  local copies, waits for them, and re-layouts  8.17 us (4%)
  waiting for transfers between devices  5.47 us (3%)
  matrix products  2.33 us (1%)
    psum x4, blocking collectives, by_axis(): shard = lax.psum(shard, axis)  62.9 us
    scatter-add x1, other arithmetic, spread(): return totals.at[:, pixel_ids].add(contribution)  56.4 us
    scatter-add x1, other arithmetic, gather_back(): return totals.at[:, cell_ids].add(contribution)  51 us
    ppermute x2, starting transfers between devices, with_halo(): lax.ppermute(head, axis, [((i + 1) % count, i) for i in range(count)])  8.83 us
    ppermute x2, starting transfers between devices, from_behind(): lax.ppermute(shard, axis, [(i, (i + by) % devices) for i in range(devices)])  5.5 us
    scatter-add x1, local copies, waits for them, and re-layouts, per_device(): own_tiles = own_part.at[:, :, tile_cols - rim_width:].add(from_east)  4.77 us
  transfers between devices with their start and end apart: 6, of which 2 were waited for; matrix products, arithmetic and copies ran while one was open for 32% of the time, Pallas kernels for 0%

commit v1 on v0

v1 whole, which is shorter than its diff:
```python
import functools
import math

import jax
import jax.numpy as jnp
from jax import lax
from jax.experimental import pallas as pl
from jax.experimental.pallas import tpu as pltpu
from jax.sharding import PartitionSpec as P

BF = jnp.bfloat16
F32 = jnp.float32
NT = (((1,), (1,)), ((), ()))
NN = (((1,), (0,)), ((), ()))
GROUPS = (8, 4, 8)


def mm(a, b, dims):
    return lax.dot_general(a, b, dims, preferred_element_type=F32)


def device_of(phase, coord, lat, lon):
    z, y = lon // 4, lon % 4
    if phase == 0:
        return (coord, lon)
    if phase == 1:
        return (lat, z * 4 + coord)
    return (lat, coord * 4 + y)


def kernel(
    scale,
    block,
    live_ref,
    latent_ref,
    head_ref,
    bias_ref,
    targets_ref,
    cell_ref,
    pixel_ref,
    weight_ref,
    grad_ref,
    head_out,
    bias_out,
    onehot_cell,
    onehot_pixel,
    west,
    east,
    from_west,
    from_east,
    cells,
    left,
    right,
    bufs0,
    bufs1,
    bufs2,
    halo_send,
    halo_recv,
    sum_send,
    sum_recv,
):
    lat = lax.axis_index("lat")
    lon = lax.axis_index("lon")
    z, y = lon // 4, lon % 4
    lon_west = lax.rem(lon + 31, 32)
    lon_east = lax.rem(lon + 1, 32)
    mine = (lat, y, z)

    barrier = pltpu.get_barrier_semaphore()
    partners = [(lat, lon_west), (lat, lon_east)]
    for phase, size in enumerate(GROUPS):
        for step in range(1, size):
            partners.append(device_of(phase, lax.rem(mine[phase] + step, size), lat, lon))
    for partner in partners:
        pl.semaphore_signal(barrier, inc=1, device_id=partner, device_id_type=pl.DeviceIdType.MESH)

    rows = cell_ref.shape[1]
    live = live_ref[0, 0]
    sub8 = lax.broadcasted_iota(jnp.int32, (8, block), 0)
    hi_iota = lax.broadcasted_iota(jnp.int32, (256, block), 0)

    repeat = (
        lax.broadcasted_iota(jnp.int32, (256, 32), 0) // 8
        == lax.broadcasted_iota(jnp.int32, (256, 32), 1)
    )
    repeat_bf = jnp.where(repeat, 1.0, 0.0).astype(BF)
    head_rep = mm(repeat_bf, head_ref[...], NN)
    bias_rep = jnp.sum(jnp.where(repeat, bias_ref[...], 0.0), axis=1, keepdims=True)
    low_of = lax.broadcasted_iota(jnp.int32, (256, 128), 0) % 8
    head_low = [jnp.where(low_of == low, head_rep, 0.0).astype(BF) for low in range(8)]

    predicted = jnp.zeros((256, 256), F32)
    for low in range(0, 8, 2):
        predicted += mm(
            jnp.concatenate([head_low[low], head_low[low + 1]], axis=1),
            jnp.concatenate([latent_ref[low], latent_ref[low + 1]], axis=1),
            NT,
        )
    predicted = (predicted + bias_rep).astype(BF)

    same_var = (
        lax.broadcasted_iota(jnp.int32, (256, 256), 0) // 8
        == lax.broadcasted_iota(jnp.int32, (256, 256), 1) // 8
    )
    collapse = jnp.where(same_var, 1.0, 0.0).astype(BF)

    def move(picked, low_from, low_to, weight):
        mask_from = jnp.where(sub8 == low_from, 1.0, 0.0)[None]
        chosen = (picked.reshape(32, 8, block) * mask_from).reshape(256, block).astype(BF)
        spread = mm(collapse, chosen, NN)
        scaled = jnp.where(sub8 == low_to, weight, 0.0)[None]
        return (spread.reshape(32, 8, block) * scaled).reshape(256, block).astype(BF)

    def row_block(step):
        span = pl.ds(pl.multiple_of(step * block, block), block)
        cell = cell_ref[:, span]
        pixel = pixel_ref[:, span]
        index = lax.broadcasted_iota(jnp.int32, (1, block), 1) + step * block
        weight = jnp.where(index < live, weight_ref[:, span], 0.0)
        return span, cell, pixel, weight

    west[...] = jnp.zeros_like(west)
    east[...] = jnp.zeros_like(east)
    rolled = pltpu.roll(targets_ref[...].astype(F32), 64, 1)
    lane = lax.broadcasted_iota(jnp.int32, (256, 128), 1)
    cells[:, :128] = jnp.where(lane >= 64, -rolled, 0.0)
    cells[:, 128:] = jnp.where(lane < 64, -rolled, 0.0)

    def forward(step, carry):
        span, cell, pixel, weight = row_block(step)
        hot_cell = jnp.where(hi_iota == (cell & 255), 1.0, 0.0).astype(BF)
        hot_pixel = jnp.where(hi_iota == (pixel & 255), 1.0, 0.0).astype(BF)
        onehot_cell[:, span] = hot_cell
        onehot_pixel[:, span] = hot_pixel
        picked = mm(predicted, hot_cell, NN)
        moved = move(picked, cell >> 8, pixel >> 8, weight)
        cells[...] += mm(moved, hot_pixel, NT)
        return carry

    lax.fori_loop(0, rows // block, forward, 0)
    west[...] = cells[:, :128].astype(BF)
    east[...] = cells[:, 128:].astype(BF)

    pl.semaphore_wait(barrier, len(partners))
    to_west = pltpu.make_async_remote_copy(
        src_ref=west,
        dst_ref=from_east,
        send_sem=halo_send.at[0],
        recv_sem=halo_recv.at[0],
        device_id=(lat, lon_west),
        device_id_type=pl.DeviceIdType.MESH,
    )
    to_east = pltpu.make_async_remote_copy(
        src_ref=east,
        dst_ref=from_west,
        send_sem=halo_send.at[1],
        recv_sem=halo_recv.at[1],
        device_id=(lat, lon_east),
        device_id_type=pl.DeviceIdType.MESH,
    )
    to_west.start()
    to_east.start()
    to_west.wait()
    to_east.wait()
    misfit = jnp.concatenate(
        [
            (cells[:, :128] + from_west[...].astype(F32)).astype(BF),
            (cells[:, 128:] + from_east[...].astype(F32)).astype(BF),
        ],
        axis=1,
    )
    cells[...] = jnp.zeros_like(cells)

    def backward(step, carry):
        span, cell, pixel, weight = row_block(step)
        picked = mm(misfit, onehot_pixel[:, span], NN)
        moved = move(picked, pixel >> 8, cell >> 8, weight)
        cells[...] += mm(moved, onehot_cell[:, span], NT)
        return carry

    lax.fori_loop(0, rows // block, backward, 0)

    left[...] = cells[:, :128]
    right[...] = cells[:, 128:]
    head_part = jnp.zeros((32, 128), F32)
    bias_part = jnp.zeros((8, 32), F32)
    ones = jnp.ones((8, 256), BF)
    for low in range(8):
        every = pl.ds(low, 32, stride=8)
        of_low = jnp.concatenate([left[every, :], right[every, :]], axis=1).astype(BF)
        head_part += mm(of_low, latent_ref[low], NN)
        bias_part += mm(ones, of_low, NT)

    all_bufs = (bufs0, bufs1, bufs2)
    total_head, total_bias = head_part, bias_part
    first = 0
    for phase, size in enumerate(GROUPS):
        bufs, me = all_bufs[phase], mine[phase]
        bufs[me, :32, :] = total_head.astype(BF)
        bufs[me, 32:, :] = jnp.zeros((16, 128), BF)
        bufs[me, 32:40, :32] = total_bias.astype(BF)
        copies = []
        for step in range(1, size):
            copy = pltpu.make_async_remote_copy(
                src_ref=bufs.at[me],
                dst_ref=bufs.at[me],
                send_sem=sum_send.at[first],
                recv_sem=sum_recv.at[first],
                device_id=device_of(phase, lax.rem(me + step, size), lat, lon),
                device_id_type=pl.DeviceIdType.MESH,
            )
            copy.start()
            copies.append(copy)
            first += 1
        if phase == 0:
            turned = cells[...].T.astype(BF)
            for low in range(8):
                grad_ref[low] = mm(turned, head_low[low], NN).astype(BF)
        for copy in copies:
            copy.wait()
        total_head = bufs[0, :32, :].astype(F32)
        total_bias = bufs[0, 32:40, :32].astype(F32)
        for other in range(1, size):
            total_head += bufs[other, :32, :].astype(F32)
            total_bias += bufs[other, 32:40, :32].astype(F32)

    head_out[...] = total_head * scale
    bias_out[...] = total_bias[:1, :] * scale


def per_device(latent, head, bias, targets, margin_cell, margin_pixel, margin_weight, live_count):
    rows = margin_cell.shape[-1]
    scale = 1.0 / math.sqrt(524288)
    block = 512
    vmem = pl.BlockSpec(memory_space=pltpu.VMEM)
    smem = pl.BlockSpec(memory_space=pltpu.SMEM)
    copies = sum(size - 1 for size in GROUPS)
    grad, head_grad, bias_grad = pl.pallas_call(
        functools.partial(kernel, scale, block),
        out_shape=(
            jax.ShapeDtypeStruct(latent.shape, BF),
            jax.ShapeDtypeStruct((32, 128), F32),
            jax.ShapeDtypeStruct((1, 32), F32),
        ),
        in_specs=[smem] + [vmem] * 7,
        out_specs=(vmem, vmem, vmem),
        scratch_shapes=[
            pltpu.VMEM((256, rows), BF),
            pltpu.VMEM((256, rows), BF),
            pltpu.VMEM((256, 128), BF),
            pltpu.VMEM((256, 128), BF),
            pltpu.VMEM((256, 128), BF),
            pltpu.VMEM((256, 128), BF),
            pltpu.VMEM((256, 256), F32),
            pltpu.VMEM((256, 128), F32),
            pltpu.VMEM((256, 128), F32),
            pltpu.VMEM((8, 48, 128), BF),
            pltpu.VMEM((4, 48, 128), BF),
            pltpu.VMEM((8, 48, 128), BF),
            pltpu.SemaphoreType.DMA((2,)),
            pltpu.SemaphoreType.DMA((2,)),
            pltpu.SemaphoreType.DMA((copies,)),
            pltpu.SemaphoreType.DMA((copies,)),
        ],
        compiler_params=pltpu.CompilerParams(
            collective_id=0, has_side_effects=True, vmem_limit_bytes=48 * 1024 * 1024
        ),
    )(
        live_count,
        latent,
        head.T,
        bias.reshape(1, 32),
        targets.reshape(256, 128),
        margin_cell.reshape(1, rows),
        margin_pixel.reshape(1, rows),
        margin_weight.reshape(1, rows),
    )
    return grad, head_grad.T, bias_grad.reshape(32)


def solution(mesh):
    lat, lon = "lat", "lon"
    in_specs = (
        P(lat, lon, None),
        P(),
        P(),
        P(None, lat, lon),
        P(lat, lon, None),
        P(lat, lon, None),
        P(lat, lon, None),
        P(lat, lon),
    )
    out_specs = (P(lat, lon, None), P(), P())
    return jax.shard_map(
        per_device, mesh=mesh, in_specs=in_specs, out_specs=out_specs, check_vma=False
    )
```

time: 208 us -> 46.4 us (0.22)
  the two profiles are of different devices: /device:TPU:4 before, /device:TPU:1 now
where the time goes in v1:
time: 46.4 us; the launch traced here: 46 us
  Pallas kernels  38 us (82%)
  local copies, waits for them, and re-layouts  6.65 us (14%)
  between operations  1.32 us (3%)
    pallas_call x1, Pallas kernels, per_device(): pl.pallas_call(functools.partial(kernel, scale, block), out_shape=(jax.Sh...  38 us
    unnamed x17, local copies, waits for them, and re-layouts  6.65 us

profile of v1, /device:TPU:1, one launch (start us, length us, event | category | flops | bytes accessed | tf_op | source)
XLA Modules:
  0.0 46.0 jit_solution(3117779515563514008)
XLA Ops:
  0.6 0.0 copy-start.5
  1.3 0.0 copy-start.6
  1.3 0.0 copy-done.5
  1.3 0.6 %copy-done.6 = f32[32]{0:T(128)S(1)} copy-done((f32[32]{0:T(128)S(1)}, f32[32]{0:T(128)}, u32[]{:S(2)}) %copy-start.6) | copy-done | bytes 152
  2.0 0.0 copy-start
  2.0 1.0 %copy-done = bf16[8,256,128]{2,1,0:T(8,128)(2,1)S(1)} copy-done((bf16[8,256,128]{2,1,0:T(8,128)(2,1)S(1)}, bf16[8,256,128]{2,1,0:T(8,128)(2,1)}, u32[]{:S(2)}) %copy-start) | copy-done | bytes 524312
  3.0 0.0 copy-start.1
  3.0 0.8 %copy-done.1 = bf16[32,8,128]{2,1,0:T(8,128)(2,1)S(1)} copy-done((bf16[32,8,128]{2,1,0:T(8,128)(2,1)S(1)}, bf16[32,8,128]{2,1,0:T(8,128)(2,1)}, u32[]{:S(2)}) %copy-start.1) | copy-done | bytes 65560
  3.8 0.0 copy-start.2
  3.8 0.7 %copy-done.2 = s32[1,1,6144]{2,1,0:T(1,128)S(1)} copy-done((s32[1,1,6144]{2,1,0:T(1,128)S(1)}, s32[1,1,6144]{2,1,0:T(1,128)}, u32[]{:S(2)}) %copy-start.2) | copy-done | bytes 24600
  4.6 0.0 copy-start.3
  4.6 0.7 %copy-done.3 = s32[1,1,6144]{2,1,0:T(1,128)S(1)} copy-done((s32[1,1,6144]{2,1,0:T(1,128)S(1)}, s32[1,1,6144]{2,1,0:T(1,128)}, u32[]{:S(2)}) %copy-start.3) | copy-done | bytes 24600
  5.3 0.0 copy-start.4
  5.3 0.7 %copy-done.4 = f32[1,1,6144]{2,1,0:T(1,128)S(1)} copy-done((f32[1,1,6144]{2,1,0:T(1,128)S(1)}, f32[1,1,6144]{2,1,0:T(1,128)}, u32[]{:S(2)}) %copy-start.4) | copy-done | bytes 24600
  6.1 38.0 %shard_map.103 = (bf16[8,256,128]{2,1,0:T(8,128)(2,1)S(1)}, f32[32,128]{1,0:T(8,128)S(1)}, f32[1,32]{1,0:T(1,128)S(1)}) custom-call(s32[1,1]{1,0:T(1,128)S(6)} %copy.14.live_ref, bf16[8,256,128]{2,1,0:T(8,128)(2,1)S(1)} %copy-done, bf16[32,128]{1,0:T(8,128)(2,1)S(1)} %bitcast.13, f32[1,32]{1,0:T(1,128)S(1)} %bitcast.14, bf16[256,128]{1,0:T(8,128)(2,1)S(1)} %bitcast.8, ...), custom_call_target="tpu_custom_call" | custom-call | tf_op jit(solution)/shard_map/pallas_call | solution.py:238
  44.1 0.8 %copy.15 = bf16[8,256,128]{2,1,0:T(8,128)(2,1)} copy(bf16[8,256,128]{2,1,0:T(8,128)(2,1)S(1)} %get-tuple-element.12) | data formatting | bytes 1048576
  44.9 0.6 %copy.16 = f32[128,32]{0,1:T(8,128)} copy(f32[128,32]{0,1:T(8,128)S(1)} %bitcast.12) | data formatting | bytes 32768
  45.5 0.5 %copy.17 = f32[32]{0:T(128)} copy(f32[32]{0:T(128)S(1)} %bitcast.15) | data formatting | bytes 256
Async XLA Ops:
  0.6 0.7 %copy-start.5 = (bf16[128,32]{0,1:T(8,128)(2,1)S(1)}, bf16[128,32]{0,1:T(8,128)(2,1)}, u32[]{:S(2)}) copy-start(bf16[128,32]{0,1:T(8,128)(2,1)} %param.9) | copy-start | bytes 24580
  1.3 0.7 %copy-start.6 = (f32[32]{0:T(128)S(1)}, f32[32]{0:T(128)}, u32[]{:S(2)}) copy-start(f32[32]{0:T(128)} %param.10) | copy-start | bytes 388
  2.0 1.0 %copy-start = (bf16[8,256,128]{2,1,0:T(8,128)(2,1)S(1)}, bf16[8,256,128]{2,1,0:T(8,128)(2,1)}, u32[]{:S(2)}) copy-start(bf16[8,256,128]{2,1,0:T(8,128)(2,1)} %latent_ref.1) | copy-start | bytes 1572868
  3.0 0.8 %copy-start.1 = (bf16[32,8,128]{2,1,0:T(8,128)(2,1)S(1)}, bf16[32,8,128]{2,1,0:T(8,128)(2,1)}, u32[]{:S(2)}) copy-start(bf16[32,8,128]{2,1,0:T(8,128)(2,1)} %param.11) | copy-start | bytes 196612
  3.8 0.7 %copy-start.2 = (s32[1,1,6144]{2,1,0:T(1,128)S(1)}, s32[1,1,6144]{2,1,0:T(1,128)}, u32[]{:S(2)}) copy-start(s32[1,1,6144]{2,1,0:T(1,128)} %param.12) | copy-start | bytes 73732
  4.6 0.7 %copy-start.3 = (s32[1,1,6144]{2,1,0:T(1,128)S(1)}, s32[1,1,6144]{2,1,0:T(1,128)}, u32[]{:S(2)}) copy-start(s32[1,1,6144]{2,1,0:T(1,128)} %param.13) | copy-start | bytes 73732
  5.3 0.7 %copy-start.4 = (f32[1,1,6144]{2,1,0:T(1,128)S(1)}, f32[1,1,6144]{2,1,0:T(1,128)}, u32[]{:S(2)}) copy-start(f32[1,1,6144]{2,1,0:T(1,128)} %param.14) | copy-start | bytes 73732

commit v2 on v1

--- a/solution.py
+++ b/solution.py
@@ -31,14 +31,14 @@
 def kernel(
     scale,
     block,
-    live_ref,
-    latent_ref,
-    head_ref,
-    bias_ref,
-    targets_ref,
-    cell_ref,
-    pixel_ref,
-    weight_ref,
+    live_in,
+    latent_in,
+    head_in,
+    bias_in,
+    targets_in,
+    cell_in,
+    pixel_in,
+    weight_in,
     grad_ref,
     head_out,
     bias_out,
@@ -58,7 +58,29 @@
     halo_recv,
     sum_send,
     sum_recv,
+    latent_ref,
+    head_ref,
+    bias_ref,
+    targets_ref,
+    cell_ref,
+    pixel_ref,
+    weight_ref,
+    load_sem,
 ):
+    pairs = (
+        (cell_in, cell_ref),
+        (pixel_in, pixel_ref),
+        (weight_in, weight_ref),
+        (head_in, head_ref),
+        (bias_in, bias_ref),
+        (latent_in, latent_ref),
+        (targets_in, targets_ref),
+    )
+    loads = []
+    for slot, (source, target) in enumerate(pairs):
+        load = pltpu.make_async_copy(source, target, load_sem.at[slot])
+        load.start()
+        loads.append(load)
     lat = lax.axis_index("lat")
     lon = lax.axis_index("lon")
     z, y = lon // 4, lon % 4
@@ -75,9 +97,12 @@
         pl.semaphore_signal(barrier, inc=1, device_id=partner, device_id_type=pl.DeviceIdType.MESH)
 
     rows = cell_ref.shape[1]
-    live = live_ref[0, 0]
     sub8 = lax.broadcasted_iota(jnp.int32, (8, block), 0)
-    hi_iota = lax.broadcasted_iota(jnp.int32, (256, block), 0)
+    hi_iota = lax.broadcasted_iota(jnp.int32, (256, block), 0).astype(F32).astype(BF)
+
+    for load in loads:
+        load.wait()
+    live = live_in[0, 0]
 
     repeat = (
         lax.broadcasted_iota(jnp.int32, (256, 32), 0) // 8
@@ -105,14 +130,22 @@
     collapse = jnp.where(same_var, 1.0, 0.0).astype(BF)
 
     def move(picked, low_from, low_to, weight):
-        mask_from = jnp.where(sub8 == low_from, 1.0, 0.0)[None]
-        chosen = (picked.reshape(32, 8, block) * mask_from).reshape(256, block).astype(BF)
-        spread = mm(collapse, chosen, NN)
-        scaled = jnp.where(sub8 == low_to, weight, 0.0)[None]
-        return (spread.reshape(32, 8, block) * scaled).reshape(256, block).astype(BF)
+        source = jnp.broadcast_to(low_from, (8, block))
+        scaled = jnp.where(sub8 == low_to, weight, 0.0)
+        return jnp.concatenate(
+            [
+                jnp.take_along_axis(picked[8 * v : 8 * v + 8], source, axis=0) * scaled
+                for v in range(32)
+            ],
+            axis=0,
+        ).astype(BF)
+
+    def hot(index):
+        high = jnp.broadcast_to((index & 255).astype(F32).astype(BF), (256, block))
+        return jnp.where(hi_iota == high, jnp.ones((), BF), jnp.zeros((), BF))
 
     def row_block(step):
-        span = pl.ds(pl.multiple_of(step * block, block), block)
+        span = pl.ds(step * block, block)
         cell = cell_ref[:, span]
         pixel = pixel_ref[:, span]
         index = lax.broadcasted_iota(jnp.int32, (1, block), 1) + step * block
@@ -128,8 +161,8 @@
 
     def forward(step, carry):
         span, cell, pixel, weight = row_block(step)
-        hot_cell = jnp.where(hi_iota == (cell & 255), 1.0, 0.0).astype(BF)
-        hot_pixel = jnp.where(hi_iota == (pixel & 255), 1.0, 0.0).astype(BF)
+        hot_cell = hot(cell)
+        hot_pixel = hot(pixel)
         onehot_cell[:, span] = hot_cell
         onehot_pixel[:, span] = hot_pixel
         picked = mm(predicted, hot_cell, NN)
@@ -137,7 +170,7 @@
         cells[...] += mm(moved, hot_pixel, NT)
         return carry
 
-    lax.fori_loop(0, rows // block, forward, 0)
+    [forward(k, 0) for k in range(rows // block)]
     west[...] = cells[:, :128].astype(BF)
     east[...] = cells[:, 128:].astype(BF)
 
@@ -178,7 +211,7 @@
         cells[...] += mm(moved, onehot_cell[:, span], NT)
         return carry
 
-    lax.fori_loop(0, rows // block, backward, 0)
+    [backward(k, 0) for k in range(rows // block)]
 
     left[...] = cells[:, :128]
     right[...] = cells[:, 128:]
@@ -228,12 +261,34 @@
     bias_out[...] = total_bias[:1, :] * scale
 
 
+def write_kernel(grad_in, head_in, bias_in, grad_out, head_out, bias_out, sem):
+    copies = []
+    for slot, (source, target) in enumerate(
+        ((grad_in, grad_out), (head_in, head_out), (bias_in, bias_out))
+    ):
+        copy = pltpu.make_async_copy(source, target, sem.at[slot])
+        copy.start()
+        copies.append(copy)
+    for copy in copies:
+        copy.wait()
+
+
+def write_out(*arrays):
+    return pl.pallas_call(
+        write_kernel,
+        out_shape=tuple(jax.ShapeDtypeStruct(a.shape, a.dtype) for a in arrays),
+        in_specs=[pl.BlockSpec(memory_space=pltpu.VMEM)] * 3,
+        out_specs=(pl.BlockSpec(memory_space=pl.ANY),) * 3,
+        scratch_shapes=[pltpu.SemaphoreType.DMA((3,))],
+        compiler_params=pltpu.CompilerParams(vmem_limit_bytes=1024 * 1024),
+    )(*arrays)
+
+
 def per_device(latent, head, bias, targets, margin_cell, margin_pixel, margin_weight, live_count):
     rows = margin_cell.shape[-1]
     scale = 1.0 / math.sqrt(524288)
     block = 512
     vmem = pl.BlockSpec(memory_space=pltpu.VMEM)
-    smem = pl.BlockSpec(memory_space=pltpu.SMEM)
     copies = sum(size - 1 for size in GROUPS)
     grad, head_grad, bias_grad = pl.pallas_call(
         functools.partial(kernel, scale, block),
@@ -242,7 +297,7 @@
             jax.ShapeDtypeStruct((32, 128), F32),
             jax.ShapeDtypeStruct((1, 32), F32),
         ),
-        in_specs=[smem] + [vmem] * 7,
+        in_specs=[pl.BlockSpec(memory_space=pltpu.SMEM)] + [pl.BlockSpec(memory_space=pltpu.HBM)] * 7,
         out_specs=(vmem, vmem, vmem),
         scratch_shapes=[
             pltpu.VMEM((256, rows), BF),
@@ -261,20 +316,34 @@
             pltpu.SemaphoreType.DMA((2,)),
             pltpu.SemaphoreType.DMA((copies,)),
             pltpu.SemaphoreType.DMA((copies,)),
+            pltpu.VMEM(latent.shape, BF),
+            pltpu.VMEM((32, 128), BF),
+            pltpu.VMEM((1, 32), F32),
+            pltpu.VMEM((256, 128), BF),
+            pltpu.VMEM((1, rows), jnp.int32),
+            pltpu.VMEM((1, rows), jnp.int32),
+            pltpu.VMEM((1, rows), F32),
+            pltpu.SemaphoreType.DMA((8,)),
         ],
         compiler_params=pltpu.CompilerParams(
-            collective_id=0, has_side_effects=True, vmem_limit_bytes=48 * 1024 * 1024
+            collective_id=0, has_side_effects=True, vmem_limit_bytes=32 * 1024 * 1024
         ),
     )(
         live_count,
-        latent,
-        head.T,
-        bias.reshape(1, 32),
-        targets.reshape(256, 128),
-        margin_cell.reshape(1, rows),
-        margin_pixel.reshape(1, rows),
-        margin_weight.reshape(1, rows),
-    )
+        *[
+            pltpu.with_memory_space_constraint(operand, pltpu.HBM)
+            for operand in (
+                latent,
+                head.T,
+                bias.reshape(1, 32),
+                targets.reshape(256, 128),
+                margin_cell.reshape(1, rows),
+                margin_pixel.reshape(1, rows),
+                margin_weight.reshape(1, rows),
+            )
+        ]
+    )
+    grad, head_grad, bias_grad = write_out(grad, head_grad, bias_grad)
     return grad, head_grad.T, bias_grad.reshape(32)
 
 

time: 46.4 us -> 30.9 us (0.67)
  Pallas kernels: 38 us -> 29.4 us
  local copies, waits for them, and re-layouts: 6.65 us -> 0 us
    pallas_call x1, Pallas kernels: 38 us -> 28.5 us  [per_device(): pl.pallas_call(functools.partial(kernel, scale, block), out_shape=(jax.Sh...]
    unnamed x17 -> x0, local copies, waits for them, and re-layouts: 6.65 us -> none
    pallas_call x0 -> x1, Pallas kernels: none -> 0.83 us  [write_out(): pl.pallas_call(write_kernel, out_shape=tuple((jax.ShapeDtypeStruct(a.shap...]
where the time goes in v2:
time: 30.9 us; the launch traced here: 30.7 us
  Pallas kernels  29.4 us (95%)
  between operations  1.29 us (4%)
    pallas_call x1, Pallas kernels, per_device(): pl.pallas_call(functools.partial(kernel, scale, block), out_shape=(jax.Sh...  28.5 us
    pallas_call x1, Pallas kernels, write_out(): pl.pallas_call(write_kernel, out_shape=tuple((jax.ShapeDtypeStruct(a.shap...  0.83 us

profile of v2, /device:TPU:1, one launch (start us, length us, event | category | flops | bytes accessed | tf_op | source)
XLA Modules:
  0.0 30.7 jit_solution(953588951925430579)
XLA Ops:
  1.3 28.5 %shard_map.103 = (bf16[8,256,128]{2,1,0:T(8,128)(2,1)S(1)}, f32[32,128]{1,0:T(8,128)S(1)}, f32[1,32]{1,0:T(1,128)S(1)}) custom-call(s32[1,1]{1,0:T(1,128)S(6)} %copy.11.live_in, bf16[8,256,128]{2,1,0:T(8,128)(2,1)} %latent_in.1, bf16[32,128]{1,0:T(8,128)(2,1)} %bitcast.12, f32[1,32]{1,0:T(1,128)} %bitcast.13, bf16[256,128]{1,0:T(8,128)(2,1)} %bitcast.8, ...), custom_call_target="tpu_custom_call" | custom-call | tf_op jit(solution)/shard_map/pallas_call | solution.py:293
  29.8 0.8 %shard_map.104 = (bf16[8,256,128]{2,1,0:T(8,128)(2,1)}, f32[32,128]{1,0:T(8,128)}, f32[1,32]{1,0:T(1,128)}) custom-call(bf16[8,256,128]{2,1,0:T(8,128)(2,1)S(1)} %get-tuple-element.9.grad_in, f32[32,128]{1,0:T(8,128)S(1)} %get-tuple-element.10.head_in, f32[1,32]{1,0:T(1,128)S(1)} %get-tuple-element.11.bias_in), custom_call_target="tpu_custom_call" | custom-call | tf_op jit(solution)/shard_map/pallas_call | solution.py:277

commit v3 on v2

--- a/solution.py
+++ b/solution.py
@@ -224,41 +224,49 @@
         head_part += mm(of_low, latent_ref[low], NN)
         bias_part += mm(ones, of_low, NT)
 
-    all_bufs = (bufs0, bufs1, bufs2)
-    total_head, total_bias = head_part, bias_part
+    bias8 = jnp.concatenate([bias_part, jnp.zeros((8, 96), F32)], axis=1)
+    total = jnp.concatenate([head_part, bias8], axis=0).reshape(5, 8, 128)
     first = 0
-    for phase, size in enumerate(GROUPS):
-        bufs, me = all_bufs[phase], mine[phase]
-        bufs[me, :32, :] = total_head.astype(BF)
-        bufs[me, 32:, :] = jnp.zeros((16, 128), BF)
-        bufs[me, 32:40, :32] = total_bias.astype(BF)
+    for phase, (bufs, size) in enumerate(zip((bufs0, bufs1, bufs2), GROUPS)):
+        me = mine[phase]
+        bufs[me] = total.astype(BF)
         copies = []
-        for step in range(1, size):
+        for order in range(size - 1):
+            other = order + jnp.where(order >= me, 1, 0)
             copy = pltpu.make_async_remote_copy(
                 src_ref=bufs.at[me],
                 dst_ref=bufs.at[me],
-                send_sem=sum_send.at[first],
-                recv_sem=sum_recv.at[first],
-                device_id=device_of(phase, lax.rem(me + step, size), lat, lon),
+                send_sem=sum_send.at[first + order],
+                recv_sem=sum_recv.at[first + me],
+                device_id=device_of(phase, other, lat, lon),
                 device_id_type=pl.DeviceIdType.MESH,
             )
             copy.start()
-            copies.append(copy)
-            first += 1
+            arrival = pltpu.make_async_remote_copy(
+                src_ref=bufs.at[other],
+                dst_ref=bufs.at[other],
+                send_sem=sum_send.at[first + order],
+                recv_sem=sum_recv.at[first + other],
+                device_id=device_of(phase, other, lat, lon),
+                device_id_type=pl.DeviceIdType.MESH,
+            )
+            copies.append((copy, arrival))
         if phase == 0:
             turned = cells[...].T.astype(BF)
             for low in range(8):
                 grad_ref[low] = mm(turned, head_low[low], NN).astype(BF)
-        for copy in copies:
-            copy.wait()
-        total_head = bufs[0, :32, :].astype(F32)
-        total_bias = bufs[0, 32:40, :32].astype(F32)
+        for copy, arrival in copies:
+            arrival.wait_recv()
+        total = bufs[0].astype(F32)
         for other in range(1, size):
-            total_head += bufs[other, :32, :].astype(F32)
-            total_bias += bufs[other, 32:40, :32].astype(F32)
-
-    head_out[...] = total_head * scale
-    bias_out[...] = total_bias[:1, :] * scale
+            total += bufs[other].astype(F32)
+        for copy, arrival in copies:
+            copy.wait_send()
+        first += size
+
+    for group in range(4):
+        head_out[8 * group : 8 * group + 8] = total[group] * scale
+    bias_out[...] = total[4][:1, :32] * scale
 
 
 def write_kernel(grad_in, head_in, bias_in, grad_out, head_out, bias_out, sem):
@@ -289,7 +297,7 @@
     scale = 1.0 / math.sqrt(524288)
     block = 512
     vmem = pl.BlockSpec(memory_space=pltpu.VMEM)
-    copies = sum(size - 1 for size in GROUPS)
+    copies = sum(GROUPS)
     grad, head_grad, bias_grad = pl.pallas_call(
         functools.partial(kernel, scale, block),
         out_shape=(
@@ -309,9 +317,9 @@
             pltpu.VMEM((256, 256), F32),
             pltpu.VMEM((256, 128), F32),
             pltpu.VMEM((256, 128), F32),
-            pltpu.VMEM((8, 48, 128), BF),
-            pltpu.VMEM((4, 48, 128), BF),
-            pltpu.VMEM((8, 48, 128), BF),
+            pltpu.VMEM((8, 5, 8, 128), BF),
+            pltpu.VMEM((4, 5, 8, 128), BF),
+            pltpu.VMEM((8, 5, 8, 128), BF),
             pltpu.SemaphoreType.DMA((2,)),
             pltpu.SemaphoreType.DMA((2,)),
             pltpu.SemaphoreType.DMA((copies,)),

time: 30.9 us -> 30.2 us (0.977)
  Pallas kernels: 29.4 us -> 28.6 us
    pallas_call x1, Pallas kernels: 28.5 us -> 27.8 us  [per_device(): pl.pallas_call(functools.partial(kernel, scale, block), out_shape=(jax.Sh...]
where the time goes in v3:
time: 30.2 us; the launch traced here: 29.9 us
  Pallas kernels  28.6 us (95%)
  between operations  1.29 us (4%)
    pallas_call x1, Pallas kernels, per_device(): pl.pallas_call(functools.partial(kernel, scale, block), out_shape=(jax.Sh...  27.8 us
    pallas_call x1, Pallas kernels, write_out(): pl.pallas_call(write_kernel, out_shape=tuple((jax.ShapeDtypeStruct(a.shap...  0.83 us

profile of v3, /device:TPU:1, one launch (start us, length us, event | category | flops | bytes accessed | tf_op | source)
XLA Modules:
  0.0 29.9 jit_solution(10201963772823396802)
XLA Ops:
  1.3 27.8 %shard_map.103 = (bf16[8,256,128]{2,1,0:T(8,128)(2,1)S(1)}, f32[32,128]{1,0:T(8,128)S(1)}, f32[1,32]{1,0:T(1,128)S(1)}) custom-call(s32[1,1]{1,0:T(1,128)S(6)} %copy.11.live_in, bf16[8,256,128]{2,1,0:T(8,128)(2,1)} %latent_in.1, bf16[32,128]{1,0:T(8,128)(2,1)} %bitcast.12, f32[1,32]{1,0:T(1,128)} %bitcast.13, bf16[256,128]{1,0:T(8,128)(2,1)} %bitcast.8, ...), custom_call_target="tpu_custom_call" | custom-call | tf_op jit(solution)/shard_map/pallas_call | solution.py:301
  29.0 0.8 %shard_map.104 = (bf16[8,256,128]{2,1,0:T(8,128)(2,1)}, f32[32,128]{1,0:T(8,128)}, f32[1,32]{1,0:T(1,128)}) custom-call(bf16[8,256,128]{2,1,0:T(8,128)(2,1)S(1)} %get-tuple-element.9.grad_in, f32[32,128]{1,0:T(8,128)S(1)} %get-tuple-element.10.head_in, f32[1,32]{1,0:T(1,128)S(1)} %get-tuple-element.11.bias_in), custom_call_target="tpu_custom_call" | custom-call | tf_op jit(solution)/shard_map/pallas_call | solution.py:285
